TPU v7x, 256 devices: a whole 4x4x8 slice. The times are simulated.
256 devices in a mesh: slab: 64 (over y, z, x_lo), ffn: 4 (over x_hi, core).
Axes of the slice: x: 4 (x_hi: 2, x_lo: 2; x = x_hi * 2 + x_lo), y: 4, z: 8, core: 2. Of those that a mesh axis runs over, the one named last changes fastest.
Arguments:
- tokens: bfloat16 [32768, 512], P('slab'), may hold values from -6 to 6
- gain_attn: float32 [512], replicated, may hold values from 0.1 to 1.9
- w_reduce: bfloat16 [4096, 512], replicated, may hold values from -0.09375 to 0.09375
- gain_keys: float32 [512], replicated, may hold values from 0.1 to 1.9
- w_query: bfloat16 [512, 512], P(None, 'ffn'), may hold values from -1.5 to 1.5
- w_key: bfloat16 [512, 512], P(None, 'ffn'), may hold values from -1.5 to 1.5
- w_value: bfloat16 [512, 512], P(None, 'ffn'), may hold values from -0.25 to 0.25
- w_out: bfloat16 [512, 512], P('ffn'), may hold values from -1.796875 to 1.796875
- gain_ffn: float32 [512], replicated, may hold values from 0.1 to 1.9
- w_up: bfloat16 [512, 2048], P(None, 'ffn'), may hold values from -0.25 to 0.25
- w_depth: float32 [27, 2048], P(None, 'ffn'), may hold values from -1.25 to 1.25
- w_down: bfloat16 [2048, 512], P('ffn'), may hold values from -0.125 to 0.125
- grad_out: bfloat16 [32768, 512], P('slab'), may hold values from -0.0625 to 0.0625
Outputs:
- attended: bfloat16 [32768, 512], P('slab')
- grad_up: float32 [512, 2048], P('slab', 'ffn')
- grad_down: float32 [512, 2048], P('slab', 'ffn')
All inputs are finite; a program needn't handle non-finite values.
Results may differ from a plain program's by a relative error of at most 0.024.
The roundings to bfloat16 on the way count: a program that leaves them out, or rounds other values in their place, can miss the bound.
Values may be sent and summed in bfloat16 or wider, within the bound.
A program may use at most 64 MiB of HBM per device.

v0:
```python
import math
import jax
import jax.numpy as jnp
from jax import lax
from jax.sharding import PartitionSpec as P

HEAD = 64
GX = 16
GY = 16
CZ = 2
EPSILON = 1e-05
ROPE_BASE = 100.0
ROOT_HALF = 0.7071067811865476
NORMAL_SCALE = 0.3989422804014327


def padded_2(cells, sides, width):
    for axis, dim in sides:
        count = lax.axis_size(axis)
        ends = count - 1
        head = lax.slice_in_dim(cells, 0, width, axis=dim)
        tail = lax.slice_in_dim(cells, cells.shape[dim] - width, cells.shape[dim], axis=dim)
        cells = jnp.concatenate(
            [
                lax.ppermute(tail, axis, [(i, (i + 1) % count) for i in range(ends)]),
                cells,
                lax.ppermute(head, axis, [((i + 1) % count, i) for i in range(ends)]),
            ],
            axis=dim,
        )
    return cells


def layer_norm(values, scale_gain):
    values = values.astype(jnp.float32)
    centered = values - jnp.mean(values, axis=-1, keepdims=True)
    variance = jnp.mean(centered * centered, axis=-1, keepdims=True)
    return centered * lax.rsqrt(variance + EPSILON) * scale_gain


def rope_tables(coord_x, coord_y, coord_z, head_size):
    pair_count = head_size // 2
    position = jnp.arange(pair_count, dtype=jnp.int32)
    axis_pick = position % 3
    per_axis = (pair_count + 2) // 3
    frequency = ROPE_BASE ** (-(position // 3).astype(jnp.float32) / per_axis)
    angles = (
        coord_x[:, None] * (axis_pick == 0)
        + coord_y[:, None] * (axis_pick == 1)
        + coord_z[:, None] * (axis_pick == 2)
    ) * frequency
    return (jnp.cos(angles)[:, None, :], jnp.sin(angles)[:, None, :])


def token_tables(first_plane, planes, head_size):
    position = jnp.arange(planes * GY * GX, dtype=jnp.int32)
    coord_x = (position % GX).astype(jnp.float32)
    coord_y = (position // GX % GY).astype(jnp.float32)
    coord_z = (first_plane + position // (GX * GY)).astype(jnp.float32)
    return rope_tables(coord_x, coord_y, coord_z, head_size)


def key_tables(first_row, row_count, head_size):
    position = first_row + jnp.arange(row_count, dtype=jnp.int32)
    half_x = GX // 2
    half_y = GY // 2
    coord_x = (position % half_x).astype(jnp.float32) * 2.0 + 0.5
    coord_y = (position // half_x % half_y).astype(jnp.float32) * 2.0 + 0.5
    coord_z = (position // (half_x * half_y)).astype(jnp.float32) * 2.0 + 0.5
    return rope_tables(coord_x, coord_y, coord_z, head_size)


def rotate(values, cosine, sine_table):
    half_size = values.shape[-1] // 2
    front_half = values[..., :half_size]
    back_half = values[..., half_size:]
    return jnp.concatenate(
        [
            front_half * cosine - back_half * sine_table,
            back_half * cosine + front_half * sine_table,
        ],
        axis=-1,
    )


def make_patches(normed, planes):
    width = normed.shape[-1]
    cell_grid = normed.reshape(planes // 2, 2, GY // 2, 2, GX // 2, 2, width)
    return cell_grid.transpose(0, 2, 4, 1, 3, 5, 6).reshape(-1, 8 * width)


def depth_conv(padded, weights, planes):
    height = padded.shape[1] - 2
    width_x = padded.shape[2] - 2
    result = jnp.zeros((planes, height, width_x, padded.shape[3]), jnp.float32)
    for offset in range(27):
        shift_z = offset // 9
        shift_y = offset // 3 % 3
        shift_x = offset % 3
        window = padded[
            shift_z : shift_z + planes, shift_y : shift_y + height, shift_x : shift_x + width_x
        ]
        result = result + window.astype(jnp.float32) * weights[offset]
    return result


def attend_piece(state_tuple, queries, key_rows, value_rows):
    row_max, row_sum, weighted = state_tuple
    score_scale = key_rows.shape[-1] ** (-0.5)
    scores = (
        jnp.einsum("qhd,khd->hqk", queries, key_rows, preferred_element_type=jnp.float32)
        * score_scale
    )
    new_max = jnp.maximum(row_max, jnp.max(scores, axis=2))
    rescale = jnp.exp(row_max - new_max)
    expo = jnp.exp(scores - new_max[:, :, None])
    row_sum = row_sum * rescale + jnp.sum(expo, axis=2)
    weighted = weighted * rescale[:, :, None] + jnp.einsum(
        "hqk,khd->hqd", expo.astype(jnp.bfloat16), value_rows, preferred_element_type=jnp.float32
    )
    return (new_max, row_sum, weighted)


def per_device(
    tokens,
    gain_attn,
    w_reduce,
    gain_keys,
    w_query,
    w_key,
    w_value,
    w_out,
    gain_ffn,
    w_up,
    w_depth,
    w_down,
    grad_out,
):
    slab_index = lax.axis_index("slab")
    tok_rows = tokens.shape[0]
    heads_dev = w_query.shape[1] // HEAD
    normed = layer_norm(tokens, gain_attn).astype(jnp.bfloat16)
    patches = make_patches(normed, CZ)
    reduced = jnp.dot(patches, w_reduce, preferred_element_type=jnp.float32)
    key_input = layer_norm(reduced, gain_keys).astype(jnp.bfloat16)
    tok_cos, tok_sin = token_tables(slab_index * CZ, CZ, HEAD)
    queries = jnp.dot(normed, w_query, preferred_element_type=jnp.float32).reshape(
        tok_rows, heads_dev, HEAD
    )
    queries = rotate(queries, tok_cos, tok_sin).astype(jnp.bfloat16)
    initial = (
        jnp.full((heads_dev, tok_rows), -1e30, jnp.float32),
        jnp.zeros((heads_dev, tok_rows), jnp.float32),
        jnp.zeros((heads_dev, tok_rows, HEAD), jnp.float32),
    )
    state_tuple = initial
    pieces = lax.all_gather(key_input, "slab", axis=0, tiled=True)
    row_count = pieces.shape[0]
    block_rows = math.gcd(row_count, 1024)
    block_count = row_count // block_rows
    blocks = pieces.reshape(block_count, block_rows, pieces.shape[1])

    def one_block(state_inner, block_item):
        rows_in, block_index = block_item
        block_first = block_index * block_rows
        key_cos, key_sin = key_tables(block_first, block_rows, HEAD)
        key_block = jnp.dot(rows_in, w_key, preferred_element_type=jnp.float32).reshape(
            block_rows, heads_dev, HEAD
        )
        key_block = rotate(key_block, key_cos, key_sin).astype(jnp.bfloat16)
        value_block = (
            jnp.dot(rows_in, w_value, preferred_element_type=jnp.float32)
            .astype(jnp.bfloat16)
            .reshape(block_rows, heads_dev, HEAD)
        )
        return (attend_piece(state_inner, queries, key_block, value_block), None)

    state_tuple, _ = lax.scan(
        one_block, state_tuple, (blocks, jnp.arange(block_count, dtype=jnp.int32))
    )
    row_max, row_sum, weighted = state_tuple
    heads_out = (
        (weighted / row_sum[:, :, None])
        .transpose(1, 0, 2)
        .reshape(tok_rows, heads_dev * HEAD)
        .astype(jnp.bfloat16)
    )
    partial_value = jnp.dot(heads_out, w_out, preferred_element_type=jnp.float32)
    head_total = lax.psum(partial_value.astype(jnp.bfloat16), "ffn").astype(jnp.float32)
    attended = head_total.astype(jnp.bfloat16)
    residual = tokens.astype(jnp.float32) + head_total
    normed_ffn = layer_norm(residual, gain_ffn).astype(jnp.bfloat16)
    channels = w_up.shape[1]
    pre = (
        jnp.dot(normed_ffn, w_up, preferred_element_type=jnp.float32)
        .astype(jnp.bfloat16)
        .reshape(CZ, GY, GX, channels)
    )
    pre_wide = padded_2(pre, (("slab", 0),), 1)
    pre_pad = jnp.pad(pre_wide, ((0, 0), (1, 1), (1, 1), (0, 0)))
    mixed = depth_conv(pre_pad, w_depth, CZ).reshape(tok_rows, channels)
    normal_cdf = 0.5 * (1.0 + lax.erf(mixed * ROOT_HALF))
    normal_pdf = jnp.exp(-0.5 * mixed * mixed) * NORMAL_SCALE
    activated = (mixed * normal_cdf).astype(jnp.bfloat16)
    grad_act = jnp.einsum("td,cd->tc", grad_out, w_down, preferred_element_type=jnp.float32)
    grad_mixed = (
        (grad_act * (normal_cdf + mixed * normal_pdf))
        .astype(jnp.bfloat16)
        .reshape(CZ, GY, GX, channels)
    )
    grad_wide = padded_2(grad_mixed, (("slab", 0),), 1)
    grad_pad = jnp.pad(grad_wide, ((0, 0), (1, 1), (1, 1), (0, 0)))
    grad_pre = (
        depth_conv(grad_pad, w_depth[::-1], CZ).astype(jnp.bfloat16).reshape(tok_rows, channels)
    )
    up_full = jnp.einsum("td,tc->dc", normed_ffn, grad_pre, preferred_element_type=jnp.float32)
    down_full = jnp.einsum("td,tc->dc", grad_out, activated, preferred_element_type=jnp.float32)
    grads = lax.psum_scatter(
        jnp.concatenate([up_full, down_full], axis=1), "slab", scatter_dimension=0, tiled=True
    )
    return (attended, grads[:, :channels], grads[:, channels:])


def solution(mesh):
    in_specs = (
        P("slab", None),
        P(),
        P(),
        P(),
        P(None, "ffn"),
        P(None, "ffn"),
        P(None, "ffn"),
        P("ffn", None),
        P(),
        P(None, "ffn"),
        P(None, "ffn"),
        P("ffn", None),
        P("slab", None),
    )
    out_specs = (P("slab", None), P("slab", "ffn"), P("slab", "ffn"))
    return jax.shard_map(
        per_device, mesh=mesh, in_specs=in_specs, out_specs=out_specs, check_vma=False
    )
```

profile of v0, /device:TPU:4, one launch (start us, length us, event | category | flops | bytes accessed | tf_op | source)
XLA Modules:
  0.0 795.7 jit_solution(1866074170113802012)
XLA Ops:
  12.2 3.2 fusion.96
  17.3 306.8 %all-gather.2.cloned.1.call-done = bf16[4096,512]{1,0:T(8,128)(2,1)} async-done(((bf16[64,512]{1,0:T(8,128)(2,1)}), bf16[4096,512]{1,0:T(8,128)(2,1)}) %all-gather.2.cloned.1.call-update) | async-done | bytes 4194320 | tf_op jit(solution)/shard_map/all_gather | solution.py:157
  324.1 48.4 %while.18 = (s32[]{:T(128)}, f32[2,512]{1,0:T(2,128)S(1)}, f32[2,512]{1,0:T(2,128)S(1)}, f32[2,512,64]{1,2,0:T(8,128)S(1)}, bf16[4,1024,512]{2,1,0:T(8,128)(2,1)...) while((s32[]{:T(128)}, f32[2,512]{1,0:T(2,128)S(1)}, ...), condition=%wide.region_7.8_spmd.clone, body=%wide.region_4.7_spmd.clone.sunk | while | flops 546895744 | bytes 35088572 | solution.py:178
  326.0 1.7 fusion.137
  327.8 2.7 bitcast_reduce_fusion.2
  330.5 3.0 fusion.143
  333.6 1.7 convolution_convert_fusion.4
  338.1 1.7 fusion.137
  339.9 2.7 bitcast_reduce_fusion.2
  342.6 3.0 fusion.143
  345.7 1.7 convolution_convert_fusion.4
  350.2 1.7 fusion.137
  352.0 2.7 bitcast_reduce_fusion.2
  354.7 3.0 fusion.143
  357.8 1.7 convolution_convert_fusion.4
  362.3 1.7 fusion.137
  364.1 2.7 bitcast_reduce_fusion.2
  366.9 3.0 fusion.143
  369.9 1.7 convolution_convert_fusion.4
  373.8 41.8 %all-reduce.4.cloned.1.call-done = bf16[512,512]{1,0:T(8,128)(2,1)} async-done(((bf16[512,512]{1,0:T(8,128)(2,1)}), bf16[512,512]{1,0:T(8,128)(2,1)}) %all-reduce.4.cloned.1.call-update) | async-done | bytes 524304 | tf_op jit(solution)/shard_map/psum | solution.py:189
  418.2 1.6 convolution_convert_fusion.1
  419.9 3.7 collective-permute-start
  425.0 10.3 %collective-permute-done = bf16[1,16,16,512]{3,2,1,0:T(8,128)(2,1)S(1)} collective-permute-done((bf16[1,16,16,512]{3,2,1,0:T(8,128)(2,1)S(1)}, bf16[1,16,16,512]{3,2,1,0:T(8,128)(2,1)S(1)}, u32[]{:S(2)}, u32[]{:S(2)}) %collective-permute-start) | collective-permute-done | bytes 262176 | tf_op jit(solution)/shard_map/ppermute | solution.py:25
  435.2 3.5 collective-permute-done.1
  439.5 3.8 multiply_add_fusion
  444.2 1.5 collective-permute-start.2
  445.7 1.5 collective-permute-start.3
  447.7 9.5 %collective-permute-done.2 = bf16[1,16,16,512]{3,2,1,0:T(8,128)(2,1)S(1)} collective-permute-done((bf16[1,16,16,512]{3,2,1,0:T(8,128)(2,1)S(1)}, bf16[1,16,16,512]{3,2,1,0:T(8,128)(2,1)S(1)}, u32[]{:S(2)}, u32[]{:S(2)}) %collective-permute-start.2) | collective-permute-done | bytes 262176 | tf_op jit(solution)/shard_map/ppermute | solution.py:25
  457.2 4.1 collective-permute-done.3
  462.1 3.8 add_convert_fusion.1
  466.8 1.8 copy.31
  468.7 318.3 %reduce-scatter.4.cloned.1.call-done = f32[8,1024]{1,0:T(8,128)} async-done(((f32[512,1024]{1,0:T(8,128)}), f32[8,1024]{1,0:T(8,128)}) %reduce-scatter.4.cloned.1.call-update) | async-done | bytes 32784
  (134 shorter events, 26.5 us)
Async XLA Ops:
  7.2 436.4 %copy-start = (bf16[512,512]{1,0:T(8,128)(2,1)S(1)}, bf16[512,512]{1,0:T(8,128)(2,1)}, u32[]{:S(2)}) copy-start(bf16[512,512]{1,0:T(8,128)(2,1)} %param.27) | copy-start | bytes 1572868
  7.2 316.9 %all-gather.2.cloned.1.call-start = ((), (), s32[]{:S(2)}) async-start(), calls=%async_computation.1 | async-start | bytes 4259840 | tf_op jit(solution)/shard_map/all_gather | solution.py:157
  11.3 4.2 copy-start.11
  11.3 5.1 copy-start.8
  11.7 5.2 copy-start.7
  12.1 311.9 %copy-start.5 = (bf16[512,128]{1,0:T(8,128)(2,1)S(1)}, bf16[512,128]{1,0:T(8,128)(2,1)}, u32[]{:S(2)}) copy-start(bf16[512,128]{1,0:T(8,128)(2,1)} %param.21) | copy-start | bytes 393220
  16.3 399.3 %all-reduce.4.cloned.1.call-start = ((), (), s32[]{:S(2)}) async-start(), calls=%async_computation.2 | async-start | bytes 1048576 | tf_op jit(solution)/shard_map/psum | solution.py:189
  324.1 48.5 %copy-start.9 = (bf16[128,512]{1,0:T(8,128)(2,1)S(1)}, bf16[128,512]{1,0:T(8,128)(2,1)}, u32[]{:S(2)}) copy-start(bf16[128,512]{1,0:T(8,128)(2,1)} %param.22) | copy-start | bytes 393220
  324.1 91.5 %copy-start.2 = (bf16[512,512]{1,0:T(8,128)(2,1)S(1)}, bf16[512,512]{1,0:T(8,128)(2,1)}, u32[]{:S(2)}) copy-start(bf16[512,512]{1,0:T(8,128)(2,1)} %param.15) | copy-start | bytes 1572868
  330.5 4.8 copy-start.1
  342.6 4.8 copy-start.1
  354.7 4.8 copy-start.1
  366.8 4.8 copy-start.1
  372.5 45.7 %copy-start.12 = (bf16[512,512]{1,0:T(8,128)(2,1)S(1)}, bf16[512,512]{1,0:T(8,128)(2,1)}, u32[]{:S(2)}) copy-start(bf16[512,512]{1,0:T(8,128)(2,1)} %param.24) | copy-start | bytes 1572868
  372.5 45.7 %copy-start.13 = (f32[512]{0:T(512)S(1)}, f32[512]{0:T(512)}, u32[]{:S(2)}) copy-start(f32[512]{0:T(512)} %param.23) | copy-start | bytes 6148
  372.6 52.3 %copy-start.10 = (f32[27,512]{1,0:T(8,128)S(1)}, f32[27,512]{1,0:T(8,128)}, u32[]{:S(2)}) copy-start(f32[27,512]{1,0:T(8,128)} %param.25) | copy-start | bytes 165892
  373.8 413.3 %reduce-scatter.4.cloned.1.call-start = ((), (), s32[]{:S(2)}) async-start(), calls=%async_computation.3 | async-start | bytes 2129920
  419.9 15.4 %collective-permute-start = (bf16[1,16,16,512]{3,2,1,0:T(8,128)(2,1)S(1)}, bf16[1,16,16,512]{3,2,1,0:T(8,128)(2,1)S(1)}, u32[]{:S(2)}, u32[]{:S(2)}) collective-permute-start(bf16[1,16,16,512]{3,2,1,0:T(8,128)(2,1)S(1)} %bitcast.133), channel_id=1, source_target_pairs={{0,4},{4,8},{8,12},{12,16},{16,20},{20,24},{24,28},{28,32},{32,36}... | collective-permute-start | bytes 786440 | tf_op jit(solution)/shard_map/ppermute | solution.py:25
  423.6 15.2 %collective-permute-start.1 = (bf16[1,16,16,512]{3,2,1,0:T(8,128)(2,1)S(1)}, bf16[1,16,16,512]{3,2,1,0:T(8,128)(2,1)S(1)}, u32[]{:S(2)}, u32[]{:S(2)}) collective-permute-start(bf16[1,16,16,512]{3,2,1,0:T(8,128)(2,1)S(1)} %bitcast.132), channel_id=1, source_target_pairs={{4,0},{8,4},{12,8},{16,12},{20,16},{24,20},{28,24},{32,28},{36,32}... | collective-permute-start | bytes 786440 | tf_op jit(solution)/shard_map/ppermute | solution.py:27
  439.5 4.1 copy-start.6
  444.2 12.9 %collective-permute-start.2 = (bf16[1,16,16,512]{3,2,1,0:T(8,128)(2,1)S(1)}, bf16[1,16,16,512]{3,2,1,0:T(8,128)(2,1)S(1)}, u32[]{:S(2)}, u32[]{:S(2)}) collective-permute-start(bf16[1,16,16,512]{3,2,1,0:T(8,128)(2,1)S(1)} %bitcast.135), channel_id=1, source_target_pairs={{0,4},{4,8},{8,12},{12,16},{16,20},{20,24},{24,28},{28,32},{32,36}... | collective-permute-start | bytes 786440 | tf_op jit(solution)/shard_map/ppermute | solution.py:25
  445.7 15.6 %collective-permute-start.3 = (bf16[1,16,16,512]{3,2,1,0:T(8,128)(2,1)S(1)}, bf16[1,16,16,512]{3,2,1,0:T(8,128)(2,1)S(1)}, u32[]{:S(2)}, u32[]{:S(2)}) collective-permute-start(bf16[1,16,16,512]{3,2,1,0:T(8,128)(2,1)S(1)} %bitcast.134), channel_id=1, source_target_pairs={{4,0},{8,4},{12,8},{16,12},{20,16},{24,20},{28,24},{32,28},{36,32}... | collective-permute-start | bytes 786440 | tf_op jit(solution)/shard_map/ppermute | solution.py:27
  462.1 3.9 copy-start.3
  466.8 321.6 %copy-start.4 = (bf16[512,512]{1,0:T(8,128)(2,1)S(1)}, bf16[512,512]{1,0:T(8,128)(2,1)}, u32[]{:S(2)}) copy-start(bf16[512,512]{1,0:T(8,128)(2,1)} %all-reduce.4.cloned.1.call-done) | copy-start | bytes 1572868
Sparse Core Ops, SparseCore 0:
  16.4 307.6 all-gather.1
  373.9 41.6 all-reduce.3
  468.8 318.1 reduce-scatter.3
where the time goes:
time: 796 us
  waiting for transfers between devices  694 us (87%)
  matrix products  35.8 us (4%)
  other arithmetic  32.5 us (4%)
  between operations  14.2 us (2%)
  starting transfers between devices  8.07 us (1%)
    unnamed x4, waiting for transfers between devices  318 us
    all_gather x1, waiting for transfers between devices, per_device(): pieces = lax.all_gather(key_input, 'slab', axis=0, tiled=True)  307 us
    psum x1, waiting for transfers between devices, per_device(): lax.psum(partial_value.astype(jnp.bfloat16), 'ffn').astype(jnp.float32)  41.8 us
    ppermute x2, waiting for transfers between devices, padded_2(): lax.ppermute(tail, axis, [(i, (i + 1) % count) for i in range(ends)])  19.8 us
  transfers between devices with their start and end apart: 7, of which 7 were waited for; matrix products, arithmetic and copies ran while one was open for 0% of the time, Pallas kernels for 0%

commit v1 on v0

--- a/solution.py
+++ b/solution.py
@@ -186,7 +186,9 @@
         .astype(jnp.bfloat16)
     )
     partial_value = jnp.dot(heads_out, w_out, preferred_element_type=jnp.float32)
-    head_total = lax.psum(partial_value.astype(jnp.bfloat16), "ffn").astype(jnp.float32)
+    head_total = jnp.sum(lax.all_gather(partial_value.astype(jnp.bfloat16), "ffn"), axis=0).astype(
+        jnp.float32
+    )
     attended = head_total.astype(jnp.bfloat16)
     residual = tokens.astype(jnp.float32) + head_total
     normed_ffn = layer_norm(residual, gain_ffn).astype(jnp.bfloat16)

time: 796 us -> 776 us (0.975)
  waiting for transfers between devices: 694 us -> 676 us
    psum x1 -> x0, waiting for transfers between devices: 41.8 us -> none  [per_device(): lax.psum(partial_value.astype(jnp.bfloat16), 'ffn').astype(jnp.float32)]
    all_gather x0 -> x1, waiting for transfers between devices: none -> 23.3 us  [per_device(): lax.all_gather(partial_value.astype(jnp.bfloat16), 'ffn')]
where the time goes in v1:
time: 776 us
  waiting for transfers between devices  676 us (87%)
  matrix products  34.8 us (4%)
  other arithmetic  32.7 us (4%)
  between operations  14.2 us (2%)
  starting transfers between devices  8.58 us (1%)
    unnamed x4, waiting for transfers between devices  318 us
    all_gather x1, waiting for transfers between devices, per_device(): pieces = lax.all_gather(key_input, 'slab', axis=0, tiled=True)  307 us
    all_gather x1, waiting for transfers between devices, per_device(): lax.all_gather(partial_value.astype(jnp.bfloat16), 'ffn')  23.3 us
    ppermute x2, waiting for transfers between devices, padded_2(): lax.ppermute(tail, axis, [(i, (i + 1) % count) for i in range(ends)])  19.7 us
  transfers between devices with their start and end apart: 7, of which 7 were waited for; matrix products, arithmetic and copies ran while one was open for 0% of the time, Pallas kernels for 0%

profile of v1, /device:TPU:4, one launch (start us, length us, event | category | flops | bytes accessed | tf_op | source)
XLA Modules:
  0.0 775.8 jit_solution(14083238668236426655)
XLA Ops:
  12.2 3.2 fusion.96
  17.3 306.8 %all-gather.4.cloned.1.call-done = bf16[4096,512]{1,0:T(8,128)(2,1)} async-done(((bf16[64,512]{1,0:T(8,128)(2,1)}), bf16[4096,512]{1,0:T(8,128)(2,1)}) %all-gather.4.cloned.1.call-update) | async-done | bytes 4194320 | tf_op jit(solution)/shard_map/all_gather | solution.py:157
  324.1 48.4 %while.18 = (s32[]{:T(128)}, f32[2,512]{1,0:T(2,128)S(1)}, f32[2,512]{1,0:T(2,128)S(1)}, f32[2,512,64]{1,2,0:T(8,128)S(1)}, bf16[4,1024,512]{2,1,0:T(8,128)(2,1)...) while((s32[]{:T(128)}, f32[2,512]{1,0:T(2,128)S(1)}, ...), condition=%wide.region_7.8_spmd.clone, body=%wide.region_4.7_spmd.clone.sunk | while | flops 546895744 | bytes 35088572 | solution.py:178
  326.0 1.7 fusion.137
  327.8 2.7 bitcast_reduce_fusion.2
  330.5 3.0 fusion.143
  333.6 1.7 convolution_convert_fusion.4
  338.1 1.7 fusion.137
  339.9 2.7 bitcast_reduce_fusion.2
  342.6 3.0 fusion.143
  345.7 1.7 convolution_convert_fusion.4
  350.2 1.7 fusion.137
  352.0 2.7 bitcast_reduce_fusion.2
  354.7 3.0 fusion.143
  357.8 1.7 convolution_convert_fusion.4
  362.3 1.7 fusion.137
  364.1 2.7 bitcast_reduce_fusion.2
  366.8 3.0 fusion.143
  369.9 1.7 convolution_convert_fusion.4
  373.8 23.3 %all-gather.6.cloned.1.call-done = bf16[2048,512]{1,0:T(8,128)(2,1)} async-done(((bf16[512,512]{1,0:T(8,128)(2,1)}), bf16[2048,512]{1,0:T(8,128)(2,1)}) %all-gather.6.cloned.1.call-update) | async-done | bytes 2097168 | tf_op jit(solution)/shard_map/all_gather | solution.py:189
  397.1 2.2 reduce_sum.83
  400.5 4.2 collective-permute-start
  406.1 10.2 %collective-permute-done = bf16[1,16,16,512]{3,2,1,0:T(8,128)(2,1)S(1)} collective-permute-done((bf16[1,16,16,512]{3,2,1,0:T(8,128)(2,1)S(1)}, bf16[1,16,16,512]{3,2,1,0:T(8,128)(2,1)S(1)}, u32[]{:S(2)}, u32[]{:S(2)}) %collective-permute-start) | collective-permute-done | bytes 262176 | tf_op jit(solution)/shard_map/ppermute | solution.py:25
  416.3 3.5 collective-permute-done.1
  420.5 3.8 multiply_add_fusion
  425.2 1.5 collective-permute-start.2
  426.7 1.5 collective-permute-start.3
  428.7 9.5 %collective-permute-done.2 = bf16[1,16,16,512]{3,2,1,0:T(8,128)(2,1)S(1)} collective-permute-done((bf16[1,16,16,512]{3,2,1,0:T(8,128)(2,1)S(1)}, bf16[1,16,16,512]{3,2,1,0:T(8,128)(2,1)S(1)}, u32[]{:S(2)}, u32[]{:S(2)}) %collective-permute-start.2) | collective-permute-done | bytes 262176 | tf_op jit(solution)/shard_map/ppermute | solution.py:25
  438.2 4.1 collective-permute-done.3
  443.1 3.8 add_convert_fusion.1
  447.9 1.8 copy.31
  449.7 318.2 %reduce-scatter.4.cloned.1.call-done = f32[8,1024]{1,0:T(8,128)} async-done(((f32[512,1024]{1,0:T(8,128)}), f32[8,1024]{1,0:T(8,128)}) %reduce-scatter.4.cloned.1.call-update) | async-done | bytes 32784
  (132 shorter events, 24.3 us)
Async XLA Ops:
  7.2 417.5 %copy-start = (bf16[512,512]{1,0:T(8,128)(2,1)S(1)}, bf16[512,512]{1,0:T(8,128)(2,1)}, u32[]{:S(2)}) copy-start(bf16[512,512]{1,0:T(8,128)(2,1)} %param.27) | copy-start | bytes 1572868
  7.2 316.9 %all-gather.4.cloned.1.call-start = ((), (), s32[]{:S(2)}) async-start(), calls=%async_computation.1 | async-start | bytes 4259840 | tf_op jit(solution)/shard_map/all_gather | solution.py:157
  11.3 4.2 copy-start.10
  11.3 5.1 copy-start.7
  11.7 5.2 copy-start.6
  12.1 311.9 %copy-start.4 = (bf16[512,128]{1,0:T(8,128)(2,1)S(1)}, bf16[512,128]{1,0:T(8,128)(2,1)}, u32[]{:S(2)}) copy-start(bf16[512,128]{1,0:T(8,128)(2,1)} %param.21) | copy-start | bytes 393220
  16.3 380.8 %all-gather.6.cloned.1.call-start = ((), (), s32[]{:S(2)}) async-start(), calls=%async_computation.2 | async-start | bytes 2621440 | tf_op jit(solution)/shard_map/all_gather | solution.py:189
  324.1 48.5 %copy-start.8 = (bf16[128,512]{1,0:T(8,128)(2,1)S(1)}, bf16[128,512]{1,0:T(8,128)(2,1)}, u32[]{:S(2)}) copy-start(bf16[128,512]{1,0:T(8,128)(2,1)} %param.22) | copy-start | bytes 393220
  330.5 4.8 copy-start.1
  342.6 4.8 copy-start.1
  354.7 4.8 copy-start.1
  366.8 4.8 copy-start.1
  372.5 26.8 %copy-start.2 = (bf16[512,512]{1,0:T(8,128)(2,1)S(1)}, bf16[512,512]{1,0:T(8,128)(2,1)}, u32[]{:S(2)}) copy-start(bf16[512,512]{1,0:T(8,128)(2,1)} %param.15) | copy-start | bytes 1572868
  372.5 27.3 %copy-start.11 = (bf16[512,512]{1,0:T(8,128)(2,1)S(1)}, bf16[512,512]{1,0:T(8,128)(2,1)}, u32[]{:S(2)}) copy-start(bf16[512,512]{1,0:T(8,128)(2,1)} %param.24) | copy-start | bytes 1572868
  372.6 27.3 %copy-start.12 = (f32[512]{0:T(512)S(1)}, f32[512]{0:T(512)}, u32[]{:S(2)}) copy-start(f32[512]{0:T(512)} %param.23) | copy-start | bytes 6148
  373.8 394.2 %reduce-scatter.4.cloned.1.call-start = ((), (), s32[]{:S(2)}) async-start(), calls=%async_computation.3 | async-start | bytes 2129920
  399.3 47.6 %copy-start.3 = (bf16[512,512]{1,0:T(8,128)(2,1)}, bf16[512,512]{1,0:T(8,128)(2,1)S(1)}, u32[]{:S(2)}) copy-start(bf16[512,512]{1,0:T(8,128)(2,1)S(1)} %reduce_sum.83) | copy-start | bytes 1572868
  399.3 6.7 copy-start.9
  400.5 15.8 %collective-permute-start = (bf16[1,16,16,512]{3,2,1,0:T(8,128)(2,1)S(1)}, bf16[1,16,16,512]{3,2,1,0:T(8,128)(2,1)S(1)}, u32[]{:S(2)}, u32[]{:S(2)}) collective-permute-start(bf16[1,16,16,512]{3,2,1,0:T(8,128)(2,1)S(1)} %bitcast.135), channel_id=1, source_target_pairs={{0,4},{4,8},{8,12},{12,16},{16,20},{20,24},{24,28},{28,32},{32,36}... | collective-permute-start | bytes 786440 | tf_op jit(solution)/shard_map/ppermute | solution.py:25
  404.7 15.0 %collective-permute-start.1 = (bf16[1,16,16,512]{3,2,1,0:T(8,128)(2,1)S(1)}, bf16[1,16,16,512]{3,2,1,0:T(8,128)(2,1)S(1)}, u32[]{:S(2)}, u32[]{:S(2)}) collective-permute-start(bf16[1,16,16,512]{3,2,1,0:T(8,128)(2,1)S(1)} %bitcast.134), channel_id=1, source_target_pairs={{4,0},{8,4},{12,8},{16,12},{20,16},{24,20},{28,24},{32,28},{36,32}... | collective-permute-start | bytes 786440 | tf_op jit(solution)/shard_map/ppermute | solution.py:27
  420.5 4.1 copy-start.5
  425.2 12.9 %collective-permute-start.2 = (bf16[1,16,16,512]{3,2,1,0:T(8,128)(2,1)S(1)}, bf16[1,16,16,512]{3,2,1,0:T(8,128)(2,1)S(1)}, u32[]{:S(2)}, u32[]{:S(2)}) collective-permute-start(bf16[1,16,16,512]{3,2,1,0:T(8,128)(2,1)S(1)} %bitcast.137), channel_id=1, source_target_pairs={{0,4},{4,8},{8,12},{12,16},{16,20},{20,24},{24,28},{28,32},{32,36}... | collective-permute-start | bytes 786440 | tf_op jit(solution)/shard_map/ppermute | solution.py:25
  426.7 15.6 %collective-permute-start.3 = (bf16[1,16,16,512]{3,2,1,0:T(8,128)(2,1)S(1)}, bf16[1,16,16,512]{3,2,1,0:T(8,128)(2,1)S(1)}, u32[]{:S(2)}, u32[]{:S(2)}) collective-permute-start(bf16[1,16,16,512]{3,2,1,0:T(8,128)(2,1)S(1)} %bitcast.136), channel_id=1, source_target_pairs={{4,0},{8,4},{12,8},{16,12},{20,16},{24,20},{28,24},{32,28},{36,32}... | collective-permute-start | bytes 786440 | tf_op jit(solution)/shard_map/ppermute | solution.py:27
Sparse Core Ops, SparseCore 0:
  16.4 307.6 all-gather.3
  373.9 23.2 all-gather.5
  449.9 318.0 reduce-scatter.3
